TPU v7x, 32 devices: a whole 2x2x4 slice. The times are simulated.
32 devices in a mesh: dp: 8 (over z, core), tensor: 4 (over y, x).
Axes of the slice: x: 2, y: 2, z: 4, core: 2. Of those that a mesh axis runs over, the one named last changes fastest.
Arguments:
- tokens: bfloat16 [16384, 2048], P(('dp', 'tensor')), may hold values from -6 to 6
- cotangent: bfloat16 [16384, 2048], P(('dp', 'tensor')), may hold values from -12 to 12
- lengths: int32 [8], P('dp'), may hold values from 512 to 2048, as said below
- query_weight: bfloat16 [2048, 2048], P('dp', 'tensor'), may hold values from -0.125 to 0.125
- key_weight: bfloat16 [2048, 2048], P('dp', 'tensor'), may hold values from -0.125 to 0.125
- value_weight: bfloat16 [2048, 2048], P('dp', 'tensor'), may hold values from -0.125 to 0.125
- out_weight: bfloat16 [2048, 2048], P('dp', 'tensor'), may hold values from -3 to 3
- up_weight: bfloat16 [2048, 8192], P('dp', 'tensor'), may hold values from -0.125 to 0.125
- down_weight: bfloat16 [2048, 8192], P('dp', 'tensor'), may hold values from -0.0625 to 0.0625
- query_bias: float32 [2048], replicated, may hold values from -1.25 to 1.25
- value_bias: float32 [2048], replicated, may hold values from -0.0625 to 0.0625
- out_bias: float32 [2048], replicated, may hold values from -0.625 to 0.625
- norm1_gain: float32 [2048], replicated, may hold values from 0.5 to 1.5
- norm1_shift: float32 [2048], replicated, may hold values from -0.625 to 0.625
- up_bias: float32 [8192], replicated, may hold values from -0.625 to 0.625
- down_bias: float32 [2048], replicated, may hold values from -0.625 to 0.625
- norm2_gain: float32 [2048], replicated, may hold values from 0.5 to 1.5
- norm2_shift: float32 [2048], replicated, may hold values from -0.625 to 0.625
Outputs:
- layer_out: bfloat16 [16384, 2048], P(('dp', 'tensor'))
- tokens_grad: bfloat16 [16384, 2048], P(('dp', 'tensor'))
- query_weight_grad: float32 [2048, 2048], P('dp', 'tensor')
- key_weight_grad: float32 [2048, 2048], P('dp', 'tensor')
- value_weight_grad: float32 [2048, 2048], P('dp', 'tensor')
- out_weight_grad: float32 [2048, 2048], P('dp', 'tensor')
- up_weight_grad: float32 [2048, 8192], P('dp', 'tensor')
- down_weight_grad: float32 [2048, 8192], P('dp', 'tensor')
- query_bias_grad: float32 [2048], P(('dp', 'tensor'))
- value_bias_grad: float32 [2048], P(('dp', 'tensor'))
- out_bias_grad: float32 [2048], P(('dp', 'tensor'))
- norm1_gain_grad: float32 [2048], P(('dp', 'tensor'))
- norm1_shift_grad: float32 [2048], P(('dp', 'tensor'))
- up_bias_grad: float32 [8192], P(('dp', 'tensor'))
- down_bias_grad: float32 [2048], P(('dp', 'tensor'))
- norm2_gain_grad: float32 [2048], P(('dp', 'tensor'))
- norm2_shift_grad: float32 [2048], P(('dp', 'tensor'))
Inputs may be any that keep to these rules, and one draw needn't show every extreme that they name: `lengths`: in every draw one slot holds a sequence of the full 2048 tokens.
All inputs are finite; a program needn't handle non-finite values.
Results may differ from a plain program's by a relative error of at most 0.025.
Values may be sent and summed in bfloat16 or wider, within the bound.
No kernel may reach another device: no remote copies, remote signals or barrier semaphores. Data moves between devices by JAX's collectives and lax.ppermute only.
A program may use at most 256 MiB of HBM per device.

v0:
```python
import jax
import jax.numpy as jnp
from jax import lax
from jax.sharding import PartitionSpec as P

HEADS = 16
HEAD_DIM = 128
FF = 8192
norm_eps = 1e-06
masked_score = -1e30


def contract_rows(left, right):
    return lax.dot_general(
        left, right, (((0,), (0,)), ((), ())), preferred_element_type=jnp.float32
    )


def contract_cols(left, right):
    return lax.dot_general(
        left, right, (((1,), (1,)), ((), ())), preferred_element_type=jnp.float32
    )


def norm_rows(value, gain, shift):
    centred = value - jnp.mean(value, axis=-1, keepdims=True)
    inverse = lax.rsqrt(jnp.mean(centred * centred, axis=-1, keepdims=True) + norm_eps)
    unit = centred * inverse
    return (unit * gain + shift, unit, inverse)


def norm_back(grad_out, unit, inverse, gain):
    grad_unit = grad_out * gain
    inner = jnp.mean(grad_unit * unit, axis=-1, keepdims=True)
    grad_in = inverse * (grad_unit - jnp.mean(grad_unit, axis=-1, keepdims=True) - unit * inner)
    return (grad_in, jnp.sum(grad_out * unit, axis=0), jnp.sum(grad_out, axis=0))


def smooth_gate(value):
    return jax.nn.gelu(value, approximate=True)


def placed(part, start, total):
    return lax.dynamic_update_slice_in_dim(jnp.zeros((total,), jnp.float32), part, start, 0)


def per_device(
    tokens,
    cotangent,
    lengths,
    query_weight,
    key_weight,
    value_weight,
    out_weight,
    up_weight,
    down_weight,
    query_bias,
    value_bias,
    out_bias,
    norm1_gain,
    norm1_shift,
    up_bias,
    down_bias,
    norm2_gain,
    norm2_shift,
):
    rows = tokens.shape[0]
    width = tokens.shape[1]
    groups = lax.axis_size("tensor")
    position = lax.axis_index("tensor")
    seq_len = rows * groups
    head_count = HEADS // groups
    head_cols = width // groups
    hidden_cols = FF // groups
    scale = HEAD_DIM ** (-0.5)
    slot_len = lengths[0]
    key_live = jnp.arange(seq_len, dtype=jnp.int32) < slot_len
    row_live = (position * rows + jnp.arange(rows, dtype=jnp.int32) < slot_len).astype(jnp.float32)[
        :, None
    ]
    col_start = position * head_cols
    hid_start = position * hidden_cols
    bias_query = lax.dynamic_slice_in_dim(query_bias, col_start, head_cols)
    bias_value = lax.dynamic_slice_in_dim(value_bias, col_start, head_cols)
    bias_up = lax.dynamic_slice_in_dim(up_bias, hid_start, hidden_cols)
    query_full, key_full, value_full, out_full = (
        lax.all_gather(query_weight, "dp", axis=0, tiled=True),
        lax.all_gather(key_weight, "dp", axis=0, tiled=True),
        lax.all_gather(value_weight, "dp", axis=0, tiled=True),
        lax.all_gather(out_weight, "dp", axis=0, tiled=True),
    )
    piece = lax.all_gather(tokens, "tensor", axis=0, tiled=True)
    queries = (jnp.dot(piece, query_full, preferred_element_type=jnp.float32) + bias_query).astype(
        jnp.bfloat16
    )
    keys = jnp.dot(piece, key_full, preferred_element_type=jnp.float32).astype(jnp.bfloat16)
    values = (jnp.dot(piece, value_full, preferred_element_type=jnp.float32) + bias_value).astype(
        jnp.bfloat16
    )
    seq_tokens, queries, keys, values = (piece, queries, keys, values)
    block = min(512, seq_len)
    blocks = seq_len // block
    key_heads = keys.reshape(seq_len, head_count, HEAD_DIM)
    value_heads = values.reshape(seq_len, head_count, HEAD_DIM)
    query_blocks = queries.reshape(blocks, block, head_count, HEAD_DIM)

    def scores_of(query_block):
        raw = (
            jnp.einsum("qhd,khd->hqk", query_block, key_heads, preferred_element_type=jnp.float32)
            * scale
        )
        return jnp.where(key_live, raw, masked_score)

    def attend(query_block):
        scores = scores_of(query_block)
        highest = jnp.max(scores, axis=-1, keepdims=True)
        normal = highest + jnp.log(jnp.sum(jnp.exp(scores - highest), axis=-1, keepdims=True))
        probs = jnp.exp(scores - normal).astype(jnp.bfloat16)
        context = jnp.einsum("hqk,khd->qhd", probs, value_heads, preferred_element_type=jnp.float32)
        return (context.astype(jnp.bfloat16), normal)

    context_blocks, totals = lax.map(attend, query_blocks)
    context = context_blocks.reshape(seq_len, head_cols)
    attn_sum = lax.psum_scatter(
        contract_cols(context, out_full).astype(jnp.bfloat16),
        "tensor",
        scatter_dimension=0,
        tiled=True,
    ).astype(jnp.float32)
    mid, mid_unit, mid_inverse = norm_rows(
        tokens.astype(jnp.float32) + attn_sum + out_bias, norm1_gain, norm1_shift
    )
    mid_low = mid.astype(jnp.bfloat16)
    up_full, down_full = (
        lax.all_gather(up_weight, "dp", axis=0, tiled=True),
        lax.all_gather(down_weight, "dp", axis=0, tiled=True),
    )
    piece = lax.all_gather(mid_low, "tensor", axis=0, tiled=True)
    pre = jnp.dot(piece, up_full, preferred_element_type=jnp.float32) + bias_up
    mid_seq = piece
    activ = smooth_gate(pre).astype(jnp.bfloat16)
    ffn_sum = lax.psum_scatter(
        contract_cols(activ, down_full).astype(jnp.bfloat16),
        "tensor",
        scatter_dimension=0,
        tiled=True,
    ).astype(jnp.float32)
    final, final_unit, final_inverse = norm_rows(mid + ffn_sum + down_bias, norm2_gain, norm2_shift)
    layer_out = (final * row_live).astype(jnp.bfloat16)
    grad_final = cotangent.astype(jnp.float32) * row_live
    grad_sum2, norm2_gain_grad, norm2_shift_grad = norm_back(
        grad_final, final_unit, final_inverse, norm2_gain
    )
    down_bias_grad = jnp.sum(grad_sum2, axis=0)
    piece = lax.all_gather(grad_sum2.astype(jnp.bfloat16), "tensor", axis=0, tiled=True)
    grad_act = jnp.dot(piece, down_full, preferred_element_type=jnp.float32)
    unused, gate_back = jax.vjp(smooth_gate, pre)
    grad_ffn = piece
    grad_pre = gate_back(grad_act)[0].astype(jnp.bfloat16)
    down_grad = contract_rows(grad_ffn, activ)
    up_grad = contract_rows(mid_seq, grad_pre)
    up_bias_part = jnp.sum(grad_pre.astype(jnp.float32), axis=0)
    grad_mid = grad_sum2 + lax.psum_scatter(
        contract_cols(grad_pre, up_full).astype(jnp.bfloat16),
        "tensor",
        scatter_dimension=0,
        tiled=True,
    ).astype(jnp.float32)
    grad_sum1, norm1_gain_grad, norm1_shift_grad = norm_back(
        grad_mid, mid_unit, mid_inverse, norm1_gain
    )
    out_bias_grad = jnp.sum(grad_sum1, axis=0)
    piece = lax.all_gather(grad_sum1.astype(jnp.bfloat16), "tensor", axis=0, tiled=True)
    grad_context = jnp.dot(piece, out_full, preferred_element_type=jnp.float32).astype(jnp.bfloat16)
    out_grad = contract_rows(piece, context)
    grad_context_blocks = grad_context.reshape(blocks, block, head_count, HEAD_DIM)

    def attend_back(carry, item):
        key_acc, value_acc = carry
        query_block, grad_block, normal = item
        probs = jnp.exp(scores_of(query_block) - normal)
        grad_probs = jnp.einsum(
            "qhd,khd->hqk", grad_block, value_heads, preferred_element_type=jnp.float32
        )
        inner = jnp.sum(probs * grad_probs, axis=-1, keepdims=True)
        grad_scores = (probs * (grad_probs - inner)).astype(jnp.bfloat16)
        grad_query = (
            jnp.einsum("hqk,khd->qhd", grad_scores, key_heads, preferred_element_type=jnp.float32)
            * scale
        )
        key_acc = (
            key_acc
            + jnp.einsum(
                "hqk,qhd->khd", grad_scores, query_block, preferred_element_type=jnp.float32
            )
            * scale
        )
        value_acc = value_acc + jnp.einsum(
            "hqk,qhd->khd",
            probs.astype(jnp.bfloat16),
            grad_block,
            preferred_element_type=jnp.float32,
        )
        return ((key_acc, value_acc), grad_query.astype(jnp.bfloat16))

    zero_heads = jnp.zeros((seq_len, head_count, HEAD_DIM), jnp.float32)
    (key_acc, value_acc), grad_query_blocks = lax.scan(
        attend_back, (zero_heads, zero_heads), (query_blocks, grad_context_blocks, totals)
    )
    grad_queries = grad_query_blocks.reshape(seq_len, head_cols)
    grad_keys = key_acc.reshape(seq_len, head_cols).astype(jnp.bfloat16)
    grad_values = value_acc.reshape(seq_len, head_cols).astype(jnp.bfloat16)
    query_grad = contract_rows(seq_tokens, grad_queries)
    key_grad = contract_rows(seq_tokens, grad_keys)
    value_grad = contract_rows(seq_tokens, grad_values)
    query_bias_part = jnp.sum(grad_queries.astype(jnp.float32), axis=0)
    value_bias_part = jnp.sum(grad_values.astype(jnp.float32), axis=0)
    total = contract_cols(grad_queries, query_full)
    total = total + contract_cols(grad_keys, key_full)
    tokens_grad = (
        grad_sum1
        + lax.psum_scatter(
            (total + contract_cols(grad_values, value_full)).astype(jnp.bfloat16),
            "tensor",
            scatter_dimension=0,
            tiled=True,
        ).astype(jnp.float32)
    ).astype(jnp.bfloat16)
    query_part, key_part, value_part, out_part, up_part, down_part = (
        lax.psum_scatter(
            query_grad.astype(jnp.bfloat16), "dp", scatter_dimension=0, tiled=True
        ).astype(jnp.float32),
        lax.psum_scatter(
            key_grad.astype(jnp.bfloat16), "dp", scatter_dimension=0, tiled=True
        ).astype(jnp.float32),
        lax.psum_scatter(
            value_grad.astype(jnp.bfloat16), "dp", scatter_dimension=0, tiled=True
        ).astype(jnp.float32),
        lax.psum_scatter(
            out_grad.astype(jnp.bfloat16), "dp", scatter_dimension=0, tiled=True
        ).astype(jnp.float32),
        lax.psum_scatter(
            up_grad.astype(jnp.bfloat16), "dp", scatter_dimension=0, tiled=True
        ).astype(jnp.float32),
        lax.psum_scatter(
            down_grad.astype(jnp.bfloat16), "dp", scatter_dimension=0, tiled=True
        ).astype(jnp.float32),
    )
    (
        query_bias_grad,
        value_bias_grad,
        out_bias_sum,
        norm1_gain_sum,
        norm1_shift_sum,
        up_bias_grad,
        down_bias_sum,
        norm2_gain_sum,
        norm2_shift_sum,
    ) = (
        lax.psum_scatter(
            placed(query_bias_part, col_start, width),
            ("dp", "tensor"),
            scatter_dimension=0,
            tiled=True,
        ),
        lax.psum_scatter(
            placed(value_bias_part, col_start, width),
            ("dp", "tensor"),
            scatter_dimension=0,
            tiled=True,
        ),
        lax.psum_scatter(out_bias_grad, ("dp", "tensor"), scatter_dimension=0, tiled=True),
        lax.psum_scatter(norm1_gain_grad, ("dp", "tensor"), scatter_dimension=0, tiled=True),
        lax.psum_scatter(norm1_shift_grad, ("dp", "tensor"), scatter_dimension=0, tiled=True),
        lax.psum_scatter(
            placed(up_bias_part, hid_start, FF), ("dp", "tensor"), scatter_dimension=0, tiled=True
        ),
        lax.psum_scatter(down_bias_grad, ("dp", "tensor"), scatter_dimension=0, tiled=True),
        lax.psum_scatter(norm2_gain_grad, ("dp", "tensor"), scatter_dimension=0, tiled=True),
        lax.psum_scatter(norm2_shift_grad, ("dp", "tensor"), scatter_dimension=0, tiled=True),
    )
    return (
        layer_out,
        tokens_grad,
        query_part,
        key_part,
        value_part,
        out_part,
        up_part,
        down_part,
        query_bias_grad,
        value_bias_grad,
        out_bias_sum,
        norm1_gain_sum,
        norm1_shift_sum,
        up_bias_grad,
        down_bias_sum,
        norm2_gain_sum,
        norm2_shift_sum,
    )


def solution(mesh):
    placed = (
        P(("dp", "tensor"), None),
        P(("dp", "tensor"), None),
        P("dp"),
        P("dp", "tensor"),
        P("dp", "tensor"),
        P("dp", "tensor"),
        P("dp", "tensor"),
        P("dp", "tensor"),
        P("dp", "tensor"),
        P(),
        P(),
        P(),
        P(),
        P(),
        P(),
        P(),
        P(),
        P(),
    )
    return jax.shard_map(
        per_device,
        mesh=mesh,
        in_specs=placed,
        out_specs=(
            P(("dp", "tensor"), None),
            P(("dp", "tensor"), None),
            P("dp", "tensor"),
            P("dp", "tensor"),
            P("dp", "tensor"),
            P("dp", "tensor"),
            P("dp", "tensor"),
            P("dp", "tensor"),
            P(("dp", "tensor")),
            P(("dp", "tensor")),
            P(("dp", "tensor")),
            P(("dp", "tensor")),
            P(("dp", "tensor")),
            P(("dp", "tensor")),
            P(("dp", "tensor")),
            P(("dp", "tensor")),
            P(("dp", "tensor")),
        ),
        check_vma=False,
    )
```

profile of v0, /device:TPU:0, one launch (start us, length us, event | category | flops | bytes accessed | tf_op | source)
XLA Modules:
  0.0 1707.2 jit_solution(15198329520281651258)
XLA Ops:
  12.2 29.3 %all-gather.17.cloned.1.call-done = bf16[2048,512]{1,0:T(8,128)(2,1)} async-done(((bf16[256,512]{1,0:T(8,128)(2,1)}), bf16[2048,512]{1,0:T(8,128)(2,1)}) %all-gather.17.cloned.1.call-update) | async-done | bytes 2097168 | tf_op jit(solution)/shard_map/all_gather | solution.py:89
  41.5 88.7 %all-gather.11.cloned.1.call-done = bf16[2048,2048]{1,0:T(8,128)(2,1)} async-done(((bf16[512,2048]{1,0:T(8,128)(2,1)}), bf16[2048,2048]{1,0:T(8,128)(2,1)}) %all-gather.11.cloned.1.call-update) | async-done | bytes 8388624 | tf_op jit(solution)/shard_map/all_gather | solution.py:92
  141.5 19.5 %all-gather.13.cloned.1.call-done = bf16[2048,512]{1,0:T(8,128)(2,1)} async-done(((bf16[256,512]{1,0:T(8,128)(2,1)}), bf16[2048,512]{1,0:T(8,128)(2,1)}) %all-gather.13.cloned.1.call-update) | async-done | bytes 2097168 | tf_op jit(solution)/shard_map/all_gather | solution.py:87
  175.1 16.0 all-gather.15.cloned.1.call-done
  204.0 87.2 %while.28 = (s32[]{:T(128)}, bf16[4,512,4,128]{3,2,1,0:T(4,128)(2,1)}, f32[4,4,512,1]{2,1,3,0:T(4,128)}, bf16[4,512,4,128]{3,1,2,0:T(8,128)(2,1)}, bf16[2048,4,1...) while((s32[]{:T(128)}, bf16[4,512,4,128]{3,2,1,0:T(4,128)(2,1)}, ...), condition=%wide.region_3.4_spmd.clone, body=%wide.region_0.3_spmd.clone.sunk | while | flops 2193883136 | bytes 132194472 | solution.py:122
  303.0 84.9 %reduce-scatter.11.cloned.1.call-done = bf16[512,2048]{1,0:T(8,128)(2,1)} async-done(((bf16[2048,2048]{1,0:T(8,128)(2,1)}), bf16[512,2048]{1,0:T(8,128)(2,1)}) %reduce-scatter.11.cloned.1.call-update) | async-done | bytes 2097168 | tf_op jit(solution)/shard_map/reduce_scatter | solution.py:124
  395.6 76.0 %all-gather.23.cloned.1.call-done = bf16[2048,2048]{1,0:T(8,128)(2,1)} async-done(((bf16[256,2048]{1,0:T(8,128)(2,1)}), bf16[2048,2048]{1,0:T(8,128)(2,1)}) %all-gather.23.cloned.1.call-update) | async-done | bytes 8388624 | tf_op jit(solution)/shard_map/all_gather | solution.py:135
  471.6 88.4 %all-gather.21.cloned.1.call-done = bf16[2048,2048]{1,0:T(8,128)(2,1)} async-done(((bf16[512,2048]{1,0:T(8,128)(2,1)}), bf16[2048,2048]{1,0:T(8,128)(2,1)}) %all-gather.21.cloned.1.call-update) | async-done | bytes 8388624 | tf_op jit(solution)/shard_map/all_gather | solution.py:138
  560.0 24.2 %fusion.64 = f32[2048,2048]{1,0:T(8,128)} fusion(bf16[2048,2048]{1,0:T(8,128)(2,1)} %all-gather.21.cloned.1.call-done, bf16[2048,2048]{1,0:T(8,128)(2,1)} %all-gather.23.cloned.1.call-done), kind=kOutput, calls=%fused_computation.124 | convolution fusion | flops 17179869184 | bytes 33554432 | tf_op jit(solution)/shard_map/dot_general | solution.py:139
  584.2 59.5 %all-gather.25.cloned.1.call-done = bf16[2048,2048]{1,0:T(8,128)(2,1)} async-done(((bf16[256,2048]{1,0:T(8,128)(2,1)}), bf16[2048,2048]{1,0:T(8,128)(2,1)}) %all-gather.25.cloned.1.call-update) | async-done | bytes 8388624 | tf_op jit(solution)/shard_map/all_gather | solution.py:136
  643.7 26.5 %convolution_convert_fusion.3 = bf16[2048,2048]{1,0:T(8,128)(2,1)} fusion(bf16[2048,2048]{1,0:T(8,128)(2,1)} %all-gather.25.cloned.1.call-done, f32[2048,2048]{1,0:T(8,128)} %fusion.64, f32[2048]{0:T(1024)S(1)} %dynamic_slice.25), kind=kOutput, calls=%fused_computation.61 | convolution fusion | flops 17226006528 | bytes 33562624 | tf_op jit(solution)/shard_map/dot_general | solution.py:20
  670.9 84.3 %reduce-scatter.13.cloned.1.call-done = bf16[512,2048]{1,0:T(8,128)(2,1)} async-done(((bf16[2048,2048]{1,0:T(8,128)(2,1)}), bf16[512,2048]{1,0:T(8,128)(2,1)}) %reduce-scatter.13.cloned.1.call-update) | async-done | bytes 2097168 | tf_op jit(solution)/shard_map/reduce_scatter | solution.py:142
  768.3 87.2 %all-gather.27.cloned.1.call-done = bf16[2048,2048]{1,0:T(8,128)(2,1)} async-done(((bf16[512,2048]{1,0:T(8,128)(2,1)}), bf16[2048,2048]{1,0:T(8,128)(2,1)}) %all-gather.27.cloned.1.call-update) | async-done | bytes 8388624 | tf_op jit(solution)/shard_map/all_gather | solution.py:155
  855.5 33.6 %convert_reduce_fusion = (f32[2048]{0:T(1024)S(1)}, bf16[2048,2048]{1,0:T(8,128)(2,1)S(1)}) fusion(f32[2048,2048]{1,0:T(8,128)} %fusion.64, f32[2048]{0:T(1024)S(1)} %dynamic_slice.25, bf16[2048,2048]{1,0:T(8,128)(2,1)} %all-gather.27.cloned.1.call-done, bf16[2048,2048]{1,0:T(8,128)(2,1)} %all-gather.25.cloned.1.call-done), kind=kOutput, calls=%fused_computation.55 | convolution fusion | flops 17276336128 | bytes 41959424 | tf_op jit(solution)/shard_map/dot_general | solution.py:156
  892.3 22.2 %convolution_convert_fusion.2 = bf16[2048,2048]{1,0:T(8,128)(2,1)} fusion(bf16[2048,2048]{1,0:T(8,128)(2,1)S(1)} %get-tuple-element.324, bf16[2048,2048]{1,0:T(8,128)(2,1)} %all-gather.23.cloned.1.call-done), kind=kOutput, calls=%fused_computation.60 | convolution fusion | flops 17184063488 | bytes 25165824 | tf_op jit(solution)/shard_map/dot_general | solution.py:20
  914.8 86.2 %reduce-scatter.15.cloned.1.call-done = bf16[512,2048]{1,0:T(8,128)(2,1)} async-done(((bf16[2048,2048]{1,0:T(8,128)(2,1)}), bf16[512,2048]{1,0:T(8,128)(2,1)}) %reduce-scatter.15.cloned.1.call-update) | async-done | bytes 2097168 | tf_op jit(solution)/shard_map/reduce_scatter | solution.py:163
  1014.8 25.1 %convolution_convert_fusion = bf16[2048,2048]{1,0:T(8,128)(2,1)} fusion(bf16[2048,2048]{1,0:T(8,128)(2,1)} %all-gather.27.cloned.1.call-done, f32[2048,2048]{1,0:T(8,128)} %fusion.64, f32[2048]{0:T(1024)S(1)} %dynamic_slice.25), kind=kOutput, calls=%fused_computation.58 | convolution fusion | flops 17226006528 | bytes 33562624 | tf_op jit(solution)/shard_map/dot_general | solution.py:14
  1042.1 23.8 %convolution_convert_fusion.1 = bf16[2048,2048]{1,0:T(8,128)(2,1)} fusion(bf16[2048,2048]{1,0:T(8,128)(2,1)} %all-gather.21.cloned.1.call-done, bf16[2048,2048]{1,0:T(8,128)(2,1)} %copy-done.27), kind=kOutput, calls=%fused_computation.59 | convolution fusion | flops 17184063488 | bytes 25165824 | tf_op jit(solution)/shard_map/dot_general | solution.py:14
  1065.9 36.4 %all-gather.29.cloned.1.call-done = bf16[2048,2048]{1,0:T(8,128)(2,1)} async-done(((bf16[512,2048]{1,0:T(8,128)(2,1)}), bf16[2048,2048]{1,0:T(8,128)(2,1)}) %all-gather.29.cloned.1.call-update) | async-done | bytes 8388624 | tf_op jit(solution)/shard_map/all_gather | solution.py:173
  1115.6 208.4 %while.29 = (s32[]{:T(128)}, f32[2048,4,128]{0,2,1:T(8,128)}, f32[2048,4,128]{0,2,1:T(8,128)}, bf16[4,512,4,128]{3,1,2,0:T(8,128)(2,1)}, bf16[4,512,4,128]{3,1,2...) while((s32[]{:T(128)}, f32[2048,4,128]{0,2,1:T(8,128)}, ...), condition=%wide.region_17.18_spmd.clone, body=%wide.region_15.17_spmd.clone.sunk | while | flops 5437390848 | bytes 253296880 | solution.py:207
  1145.6 12.4 multiply_convert_fusion.6
  1197.9 12.9 multiply_convert_fusion.6
  1238.6 12.3 multiply_reduce_fusion.9
  1250.8 12.3 multiply_convert_fusion.6
  1375.6 12.7 fusion.65
  1396.6 17.1 %add_convert_fusion = bf16[2048,2048]{1,0:T(8,128)(2,1)} fusion(f32[2048,2048]{1,0:T(8,128)} %fusion.50, f32[2048,2048]{1,0:T(8,128)} %fusion.65, bf16[2048,512]{0,1:T(8,128)(2,1)S(1)} %bitcast.138, bf16[2048,512]{1,0:T(8,128)(2,1)} %all-gather.17.cloned.1.call-done), kind=kOutput, calls=%fused_computation.56 | convolution fusion | flops 4307550208 | bytes 46137344 | tf_op jit(solution)/shard_map/dot_general | solution.py:20
  1419.4 37.2 %all-reduce.12.cloned.1.call-done = (f32[2048]{0:T(1024)}, f32[2048]{0:T(1024)}, f32[2048]{0:T(1024)}, f32[2048]{0:T(1024)}, f32[2048]{0:T(1024)}, /*index=5*/f3...) async-done(((f32[2048]{0:T(1024)}, f32[2048]{0:T(1024)}, f32[2048]{0:T(1024)}, f32[2048]{0:T(1024)}, f32[2048]{0:T(1024)}, /*index=5*/f32[8192]{0:T(1024)}, ...) | async-done | bytes 98320
  1468.0 27.9 %reduce-scatter.25.cloned.1.call-done = bf16[256,512]{1,0:T(8,128)(2,1)} async-done(((bf16[2048,512]{1,0:T(8,128)(2,1)}), bf16[256,512]{1,0:T(8,128)(2,1)}) %reduce-scatter.25.cloned.1.call-update) | async-done | bytes 262160 | tf_op jit(solution)/shard_map/reduce_scatter | solution.py:239
  1497.7 35.6 %reduce-scatter.19.cloned.1.call-done = bf16[256,512]{0,1:T(8,128)(2,1)} async-done(((bf16[2048,512]{0,1:T(8,128)(2,1)}), bf16[256,512]{0,1:T(8,128)(2,1)}) %reduce-scatter.19.cloned.1.call-update) | async-done | bytes 262160 | tf_op jit(solution)/shard_map/reduce_scatter | solution.py:230
  1535.2 35.1 %reduce-scatter.21.cloned.1.call-done = bf16[256,512]{0,1:T(8,128)(2,1)} async-done(((bf16[2048,512]{0,1:T(8,128)(2,1)}), bf16[256,512]{0,1:T(8,128)(2,1)}) %reduce-scatter.21.cloned.1.call-update) | async-done | bytes 262160 | tf_op jit(solution)/shard_map/reduce_scatter | solution.py:233
  1572.2 34.9 %reduce-scatter.23.cloned.1.call-done = bf16[256,512]{0,1:T(8,128)(2,1)} async-done(((bf16[2048,512]{0,1:T(8,128)(2,1)}), bf16[256,512]{0,1:T(8,128)(2,1)}) %reduce-scatter.23.cloned.1.call-update) | async-done | bytes 262160 | tf_op jit(solution)/shard_map/reduce_scatter | solution.py:236
  1609.0 86.2 %reduce-scatter.17.cloned.1.call-done = bf16[512,2048]{1,0:T(8,128)(2,1)} async-done(((bf16[2048,2048]{1,0:T(8,128)(2,1)}), bf16[512,2048]{1,0:T(8,128)(2,1)}) %reduce-scatter.17.cloned.1.call-update) | async-done | bytes 2097168 | tf_op jit(solution)/shard_map/reduce_scatter | solution.py:222
  (254 shorter events, 441.8 us)
Async XLA Ops:
  7.2 34.3 %all-gather.17.cloned.1.call-start = ((), (), s32[]{:S(2)}) async-start(), calls=%async_computation.13 | async-start | bytes 2359296 | tf_op jit(solution)/shard_map/all_gather | solution.py:89
  7.9 122.3 %all-gather.11.cloned.1.call-start = ((), (), s32[]{:S(2)}) async-start(), calls=%async_computation.10 | async-start | bytes 10485760 | tf_op jit(solution)/shard_map/all_gather | solution.py:92
  8.7 152.4 %all-gather.13.cloned.1.call-start = ((), (), s32[]{:S(2)}) async-start(), calls=%async_computation.11 | async-start | bytes 2359296 | tf_op jit(solution)/shard_map/all_gather | solution.py:87
  9.4 181.7 %all-gather.15.cloned.1.call-start = ((), (), s32[]{:S(2)}) async-start(), calls=%async_computation.12 | async-start | bytes 2359296 | tf_op jit(solution)/shard_map/all_gather | solution.py:88
  10.0 281.2 %all-gather.19.cloned.1.call-start = ((), (), s32[]{:S(2)}) async-start(), calls=%async_computation.14 | async-start | bytes 2359296 | tf_op jit(solution)/shard_map/all_gather | solution.py:90
  10.6 377.3 %reduce-scatter.11.cloned.1.call-start = ((), (), s32[]{:S(2)}) async-start(), calls=%async_computation.15 | async-start | bytes 10485760 | tf_op jit(solution)/shard_map/reduce_scatter | solution.py:124
  208.8 7.0 copy-start.4
  291.2 10.8 copy-start.2
  302.0 85.9 %copy-start.7 = (bf16[512,2048]{1,0:T(8,128)(2,1)S(1)}, bf16[512,2048]{1,0:T(8,128)(2,1)}, u32[]{:S(2)}) copy-start(bf16[512,2048]{1,0:T(8,128)(2,1)} %param.22) | copy-start | bytes 6291460
  302.0 85.9 %copy-start.17 = (f32[2048]{0:T(1024)S(1)}, f32[2048]{0:T(1024)}, u32[]{:S(2)}) copy-start(f32[2048]{0:T(1024)} %param.33) | copy-start | bytes 24580
  302.0 169.6 %all-gather.23.cloned.1.call-start = ((), (), s32[]{:S(2)}) async-start(), calls=%async_computation.17 | async-start | bytes 9437184 | tf_op jit(solution)/shard_map/all_gather | solution.py:135
  302.8 88.7 %copy-start.18 = (f32[2048]{0:T(1024)S(1)}, f32[2048]{0:T(1024)}, u32[]{:S(2)}) copy-start(f32[2048]{0:T(1024)} %param.34) | copy-start | bytes 24580
  302.8 88.7 %copy-start.22 = (f32[2048]{0:T(1024)S(1)}, f32[2048]{0:T(1024)}, u32[]{:S(2)}) copy-start(f32[2048]{0:T(1024)} %param.35) | copy-start | bytes 24580
  302.8 257.2 %all-gather.21.cloned.1.call-start = ((), (), s32[]{:S(2)}) async-start(), calls=%async_computation.16 | async-start | bytes 10485760 | tf_op jit(solution)/shard_map/all_gather | solution.py:138
  394.1 249.6 %all-gather.25.cloned.1.call-start = ((), (), s32[]{:S(2)}) async-start(), calls=%async_computation.18 | async-start | bytes 9437184 | tf_op jit(solution)/shard_map/all_gather | solution.py:136
  394.8 360.4 %reduce-scatter.13.cloned.1.call-start = ((), (), s32[]{:S(2)}) async-start(), calls=%async_computation.19 | async-start | bytes 10485760 | tf_op jit(solution)/shard_map/reduce_scatter | solution.py:142
  670.2 85.0 %copy-start.24 = (f32[2048]{0:T(1024)S(1)}, f32[2048]{0:T(1024)}, u32[]{:S(2)}) copy-start(f32[2048]{0:T(1024)} %param.37) | copy-start | bytes 24580
  670.2 185.2 %all-gather.27.cloned.1.call-start = ((), (), s32[]{:S(2)}) async-start(), calls=%async_computation.20 | async-start | bytes 10485760 | tf_op jit(solution)/shard_map/all_gather | solution.py:155
  767.8 233.2 %reduce-scatter.15.cloned.1.call-start = ((), (), s32[]{:S(2)}) async-start(), calls=%async_computation.21 | async-start | bytes 10485760 | tf_op jit(solution)/shard_map/reduce_scatter | solution.py:163
  914.5 187.8 %all-gather.29.cloned.1.call-start = ((), (), s32[]{:S(2)}) async-start(), calls=%async_computation.22 | async-start | bytes 10485760 | tf_op jit(solution)/shard_map/all_gather | solution.py:173
  1001.0 7.0 copy-start.12
  1014.7 399.0 %reduce-scatter.29.cloned.1.call-start = ((), (), s32[]{:S(2)}) async-start(), calls=%async_computation.29 | async-start | bytes 9437184 | tf_op jit(solution)/shard_map/reduce_scatter | solution.py:245
  1039.9 376.7 %reduce-scatter.27.cloned.1.call-start = ((), (), s32[]{:S(2)}) async-start(), calls=%async_computation.28 | async-start | bytes 9437184 | tf_op jit(solution)/shard_map/reduce_scatter | solution.py:242
  1065.8 36.5 %copy-start.26 = (bf16[2048,512]{1,0:T(8,128)(2,1)S(1)}, bf16[2048,512]{1,0:T(8,128)(2,1)}, u32[]{:S(2)}) copy-start(bf16[2048,512]{1,0:T(8,128)(2,1)} %all-gather.19.cloned.1.call-done) | copy-start | bytes 6291460
  1065.9 390.7 %all-reduce.12.cloned.1.call-start = ((), (), s32[]{:S(2)}) async-start(), calls=%async_computation.30 | async-start | bytes 196608
  1329.2 166.7 %reduce-scatter.25.cloned.1.call-start = ((), (), s32[]{:S(2)}) async-start(), calls=%async_computation.27 | async-start | bytes 2359296 | tf_op jit(solution)/shard_map/reduce_scatter | solution.py:239
  1339.2 194.2 %reduce-scatter.19.cloned.1.call-start = ((), (), s32[]{:S(2)}) async-start(), calls=%async_computation.24 | async-start | bytes 2359296 | tf_op jit(solution)/shard_map/reduce_scatter | solution.py:230
  1353.0 217.3 %reduce-scatter.21.cloned.1.call-start = ((), (), s32[]{:S(2)}) async-start(), calls=%async_computation.25 | async-start | bytes 2359296 | tf_op jit(solution)/shard_map/reduce_scatter | solution.py:233
  1366.1 241.0 %reduce-scatter.23.cloned.1.call-start = ((), (), s32[]{:S(2)}) async-start(), calls=%async_computation.26 | async-start | bytes 2359296 | tf_op jit(solution)/shard_map/reduce_scatter | solution.py:236
  1375.5 319.7 %reduce-scatter.17.cloned.1.call-start = ((), (), s32[]{:S(2)}) async-start(), calls=%async_computation.23 | async-start | bytes 10485760 | tf_op jit(solution)/shard_map/reduce_scatter | solution.py:222
  1375.6 12.7 copy-start.16
  1375.6 12.7 copy-start.25
  (32 other events, 128.3 us)
Sparse Core Ops, SparseCore 0:
  9.6 31.8 all-gather.16
  43.3 86.8 all-gather.10
  131.9 29.1 all-gather.12
  162.5 28.5 all-gather.14
  192.5 28.5 all-gather.18
  302.1 85.7 reduce-scatter.10
  389.5 82.0 all-gather.22
  474.0 85.9 all-gather.20
  561.6 82.0 all-gather.24
  670.3 84.7 reduce-scatter.12
  768.0 87.4 all-gather.26
  914.7 86.3 reduce-scatter.14
  1014.8 87.4 all-gather.28
  1104.5 89.5 reduce-scatter.28
  1196.2 87.9 reduce-scatter.26
  1329.4 127.2 all-reduce.11
  1458.7 37.1 reduce-scatter.24
  1498.6 34.6 reduce-scatter.18
  1535.6 34.6 reduce-scatter.20
  1572.5 34.5 reduce-scatter.22
  1610.2 84.9 reduce-scatter.16
where the time goes:
time: 1710 us
  waiting for transfers between devices  1020 us (60%)
  matrix products  448 us (26%)
  other arithmetic  121 us (7%)
  local copies, waits for them, and re-layouts  102 us (6%)
    dot_general x6, matrix products, contract_cols(): lax.dot_general(left, right, (((1,), (1,)), ((), ())), preferred_element_...  97.6 us
    all_gather x1, waiting for transfers between devices, per_device(): piece = lax.all_gather(tokens, 'tensor', axis=0, tiled=True)  88.7 us
    all_gather x1, waiting for transfers between devices, per_device(): piece = lax.all_gather(mid_low, 'tensor', axis=0, tiled=True)  88.4 us
    all_gather x1, waiting for transfers between devices, per_device(): lax.all_gather(grad_sum2.astype(jnp.bfloat16), 'tensor', axis=0, tiled=True)  87.2 us
    dot_general x6, matrix products, contract_rows(): lax.dot_general(left, right, (((0,), (0,)), ((), ())), preferred_element_...  86.5 us
    reduce_scatter x1, waiting for transfers between devices, per_device(): lax.psum_scatter(contract_cols(grad_pre, up_full).astype(jnp.bfloat16), '...  86.2 us
    reduce_scatter x1, waiting for transfers between devices, per_device(): lax.psum_scatter((total + contract_cols(grad_values, value_full)).astype(...  86.2 us
    reduce_scatter x1, waiting for transfers between devices, per_device(): lax.psum_scatter(contract_cols(context, out_full).astype(jnp.bfloat16), '...  84.9 us
  transfers between devices with their start and end apart: 21, of which 18 were waited for; matrix products, arithmetic and copies ran while one was open for 29% of the time, Pallas kernels for 0%

commit v1 on v0

--- a/solution.py
+++ b/solution.py
@@ -8,6 +8,12 @@
 FF = 8192
 norm_eps = 1e-06
 masked_score = -1e30
+
+
+def in_order(blocks, dim):
+    shape = list(blocks.shape[1:])
+    shape[dim] *= blocks.shape[0]
+    return jnp.moveaxis(blocks, 0, dim).reshape(shape)
 
 
 def contract_rows(left, right):
@@ -135,7 +141,19 @@
         lax.all_gather(up_weight, "dp", axis=0, tiled=True),
         lax.all_gather(down_weight, "dp", axis=0, tiled=True),
     )
-    piece = lax.all_gather(mid_low, "tensor", axis=0, tiled=True)
+    size = lax.axis_size("tensor")
+    pairs = [(i, (i + 1) % size) for i in range(size)]
+    back = [(b, a) for a, b in pairs]
+    lower, upper = ([], [])
+    for step in range(size - 1):
+        if step % 2 == 0:
+            lower.append(lax.ppermute(lower[-1] if lower else mid_low, "tensor", pairs))
+        else:
+            upper.append(lax.ppermute(upper[-1] if upper else mid_low, "tensor", back))
+    tiles = jnp.stack([*lower[::-1], mid_low, *upper])
+    shift_2 = lax.axis_index("tensor") - len(lower)
+    tiles = tiles[(jnp.arange(size) - shift_2) % size]
+    piece = in_order(tiles, 0)
     pre = jnp.dot(piece, up_full, preferred_element_type=jnp.float32) + bias_up
     mid_seq = piece
     activ = smooth_gate(pre).astype(jnp.bfloat16)

time: 1710 us -> 1650 us (0.965)
  waiting for transfers between devices: 1020 us -> 929 us
    ppermute x0 -> x3, waiting for transfers between devices: none -> 134 us  [the longest x2 90.4 us: per_device(): lower.append(lax.ppermute(lower[-1] if lower else mid_low, 'tensor', pairs))]
    all_gather x1 -> x0, waiting for transfers between devices: 88.4 us -> none  [per_device(): piece = lax.all_gather(mid_low, 'tensor', axis=0, tiled=True)]
    all_gather x1, waiting for transfers between devices: 76 us -> 0.01 us  [per_device(): lax.all_gather(up_weight, 'dp', axis=0, tiled=True)]
    all_gather x1, waiting for transfers between devices: 59.5 us -> 0.01 us  [per_device(): lax.all_gather(down_weight, 'dp', axis=0, tiled=True)]
    unnamed x22 -> x21, waiting for transfers between devices: 42 us -> 41.9 us
  transfers between devices with their start and end apart: 21 -> 23, of which waited for: 18 -> 18; matrix products, arithmetic and copies ran while one was open for 29% -> 32% of each run, Pallas kernels for 0% -> 0%
where the time goes in v1:
time: 1650 us
  waiting for transfers between devices  929 us (56%)
  matrix products  448 us (27%)
  other arithmetic  133 us (8%)
  local copies, waits for them, and re-layouts  116 us (7%)
    dot_general x6, matrix products, contract_cols(): lax.dot_general(left, right, (((1,), (1,)), ((), ())), preferred_element_...  97.6 us
    ppermute x2, waiting for transfers between devices, per_device(): lower.append(lax.ppermute(lower[-1] if lower else mid_low, 'tensor', pairs))  90.4 us
    all_gather x1, waiting for transfers between devices, per_device(): piece = lax.all_gather(tokens, 'tensor', axis=0, tiled=True)  88.7 us
    all_gather x1, waiting for transfers between devices, per_device(): lax.all_gather(grad_sum2.astype(jnp.bfloat16), 'tensor', axis=0, tiled=True)  87.6 us
    dot_general x6, matrix products, contract_rows(): lax.dot_general(left, right, (((0,), (0,)), ((), ())), preferred_element_...  86.6 us
    reduce_scatter x1, waiting for transfers between devices, per_device(): lax.psum_scatter(contract_cols(grad_pre, up_full).astype(jnp.bfloat16), '...  86 us
    reduce_scatter x1, waiting for transfers between devices, per_device(): lax.psum_scatter((total + contract_cols(grad_values, value_full)).astype(...  85.9 us
    reduce_scatter x1, waiting for transfers between devices, per_device(): lax.psum_scatter(contract_cols(activ, down_full).astype(jnp.bfloat16), 't...  85.6 us
  transfers between devices with their start and end apart: 23, of which 18 were waited for; matrix products, arithmetic and copies ran while one was open for 32% of the time, Pallas kernels for 0%

profile of v1, /device:TPU:0, one launch (start us, length us, event | category | flops | bytes accessed | tf_op | source)
XLA Modules:
  0.0 1648.4 jit_solution(9310466015903434492)
XLA Ops:
  12.2 29.3 %all-gather.16.cloned.1.call-done = bf16[2048,512]{1,0:T(8,128)(2,1)} async-done(((bf16[256,512]{1,0:T(8,128)(2,1)}), bf16[2048,512]{1,0:T(8,128)(2,1)}) %all-gather.16.cloned.1.call-update) | async-done | bytes 2097168 | tf_op jit(solution)/shard_map/all_gather | solution.py:95
  41.5 88.7 %all-gather.10.cloned.1.call-done = bf16[2048,2048]{1,0:T(8,128)(2,1)} async-done(((bf16[512,2048]{1,0:T(8,128)(2,1)}), bf16[2048,2048]{1,0:T(8,128)(2,1)}) %all-gather.10.cloned.1.call-update) | async-done | bytes 8388624 | tf_op jit(solution)/shard_map/all_gather | solution.py:98
  141.5 19.5 %all-gather.12.cloned.1.call-done = bf16[2048,512]{1,0:T(8,128)(2,1)} async-done(((bf16[256,512]{1,0:T(8,128)(2,1)}), bf16[2048,512]{1,0:T(8,128)(2,1)}) %all-gather.12.cloned.1.call-update) | async-done | bytes 2097168 | tf_op jit(solution)/shard_map/all_gather | solution.py:93
  175.1 16.0 all-gather.14.cloned.1.call-done
  204.0 87.0 %while.28 = (s32[]{:T(128)}, bf16[4,512,4,128]{3,2,1,0:T(4,128)(2,1)}, f32[4,4,512,1]{2,1,3,0:T(4,128)}, bf16[4,512,4,128]{3,1,2,0:T(8,128)(2,1)}, bf16[2048,4,1...) while((s32[]{:T(128)}, bf16[4,512,4,128]{3,2,1,0:T(4,128)(2,1)}, ...), condition=%wide.region_3.4_spmd.clone, body=%wide.region_0.3_spmd.clone.sunk | while | flops 2193883136 | bytes 132194472 | solution.py:128
  303.9 83.8 %reduce-scatter.11.cloned.1.call-done = bf16[512,2048]{1,0:T(8,128)(2,1)} async-done(((bf16[2048,2048]{1,0:T(8,128)(2,1)}), bf16[512,2048]{1,0:T(8,128)(2,1)}) %reduce-scatter.11.cloned.1.call-update) | async-done | bytes 2097168 | tf_op jit(solution)/shard_map/reduce_scatter | solution.py:130
  396.8 46.8 %collective-permute-done = bf16[512,2048]{1,0:T(8,128)(2,1)} collective-permute-done((bf16[512,2048]{1,0:T(8,128)(2,1)}, bf16[512,2048]{1,0:T(8,128)(2,1)}, u32[]{:S(2)}, u32[]{:S(2)}) %collective-permute-start) | collective-permute-done | bytes 2097184 | tf_op jit(solution)/shard_map/ppermute | solution.py:150
  444.9 43.6 %collective-permute-done.2 = bf16[512,2048]{1,0:T(8,128)(2,1)} collective-permute-done((bf16[512,2048]{1,0:T(8,128)(2,1)}, bf16[512,2048]{1,0:T(8,128)(2,1)}, u32[]{:S(2)}, u32[]{:S(2)}) %collective-permute-start.2) | collective-permute-done | bytes 2097184 | tf_op jit(solution)/shard_map/ppermute | solution.py:152
  488.5 43.7 %collective-permute-done.1 = bf16[512,2048]{1,0:T(8,128)(2,1)} collective-permute-done((bf16[512,2048]{1,0:T(8,128)(2,1)}, bf16[512,2048]{1,0:T(8,128)(2,1)}, u32[]{:S(2)}, u32[]{:S(2)}) %collective-permute-start.1) | collective-permute-done | bytes 2097184 | tf_op jit(solution)/shard_map/ppermute | solution.py:150
  558.4 24.2 %fusion.67 = f32[2048,2048]{1,0:T(8,128)} fusion(bf16[2048,2048]{1,0:T(8,128)(2,1)} %bitcast.146, bf16[2048,2048]{1,0:T(8,128)(2,1)} %all-gather.20.cloned.1.call-done), kind=kOutput, calls=%fused_computation.136 | convolution fusion | flops 17179869184 | bytes 33554432 | tf_op jit(solution)/shard_map/dot_general | solution.py:157
  582.6 26.5 %convolution_convert_fusion.3 = bf16[2048,2048]{1,0:T(8,128)(2,1)} fusion(bf16[2048,2048]{1,0:T(8,128)(2,1)} %all-gather.22.cloned.1.call-done, f32[2048,2048]{1,0:T(8,128)} %fusion.67, f32[2048]{0:T(1024)S(1)} %dynamic_slice.25), kind=kOutput, calls=%fused_computation.65 | convolution fusion | flops 17226006528 | bytes 33562624 | tf_op jit(solution)/shard_map/dot_general | solution.py:26
  610.1 85.6 %reduce-scatter.13.cloned.1.call-done = bf16[512,2048]{1,0:T(8,128)(2,1)} async-done(((bf16[2048,2048]{1,0:T(8,128)(2,1)}), bf16[512,2048]{1,0:T(8,128)(2,1)}) %reduce-scatter.13.cloned.1.call-update) | async-done | bytes 2097168 | tf_op jit(solution)/shard_map/reduce_scatter | solution.py:160
  708.4 87.6 %all-gather.24.cloned.1.call-done = bf16[2048,2048]{1,0:T(8,128)(2,1)} async-done(((bf16[512,2048]{1,0:T(8,128)(2,1)}), bf16[2048,2048]{1,0:T(8,128)(2,1)}) %all-gather.24.cloned.1.call-update) | async-done | bytes 8388624 | tf_op jit(solution)/shard_map/all_gather | solution.py:173
  796.0 33.6 %convert_reduce_fusion = (f32[2048]{0:T(1024)S(1)}, bf16[2048,2048]{1,0:T(8,128)(2,1)S(1)}) fusion(f32[2048,2048]{1,0:T(8,128)} %fusion.67, f32[2048]{0:T(1024)S(1)} %dynamic_slice.25, bf16[2048,2048]{1,0:T(8,128)(2,1)} %all-gather.24.cloned.1.call-done, bf16[2048,2048]{1,0:T(8,128)(2,1)} %all-gather.22.cloned.1.call-done), kind=kOutput, calls=%fused_computation.57 | convolution fusion | flops 17276336128 | bytes 41959424 | tf_op jit(solution)/shard_map/dot_general | solution.py:174
  833.0 22.2 %convolution_convert_fusion.2 = bf16[2048,2048]{1,0:T(8,128)(2,1)} fusion(bf16[2048,2048]{1,0:T(8,128)(2,1)S(1)} %get-tuple-element.324, bf16[2048,2048]{1,0:T(8,128)(2,1)} %all-gather.20.cloned.1.call-done), kind=kOutput, calls=%fused_computation.64 | convolution fusion | flops 17184063488 | bytes 25165824 | tf_op jit(solution)/shard_map/dot_general | solution.py:26
  855.6 86.0 %reduce-scatter.15.cloned.1.call-done = bf16[512,2048]{1,0:T(8,128)(2,1)} async-done(((bf16[2048,2048]{1,0:T(8,128)(2,1)}), bf16[512,2048]{1,0:T(8,128)(2,1)}) %reduce-scatter.15.cloned.1.call-update) | async-done | bytes 2097168 | tf_op jit(solution)/shard_map/reduce_scatter | solution.py:181
  955.4 25.1 %convolution_convert_fusion = bf16[2048,2048]{1,0:T(8,128)(2,1)} fusion(bf16[2048,2048]{1,0:T(8,128)(2,1)} %all-gather.24.cloned.1.call-done, f32[2048,2048]{1,0:T(8,128)} %fusion.67, f32[2048]{0:T(1024)S(1)} %dynamic_slice.25), kind=kOutput, calls=%fused_computation.62 | convolution fusion | flops 17226006528 | bytes 33562624 | tf_op jit(solution)/shard_map/dot_general | solution.py:20
  982.7 23.8 %convolution_convert_fusion.1 = bf16[2048,2048]{1,0:T(8,128)(2,1)} fusion(bf16[2048,2048]{1,0:T(8,128)(2,1)} %bitcast.147, bf16[2048,2048]{1,0:T(8,128)(2,1)} %copy-done.27), kind=kOutput, calls=%fused_computation.63 | convolution fusion | flops 17184063488 | bytes 25165824 | tf_op jit(solution)/shard_map/dot_general | solution.py:20
  1006.5 36.4 %all-gather.26.cloned.1.call-done = bf16[2048,2048]{1,0:T(8,128)(2,1)} async-done(((bf16[512,2048]{1,0:T(8,128)(2,1)}), bf16[2048,2048]{1,0:T(8,128)(2,1)}) %all-gather.26.cloned.1.call-update) | async-done | bytes 8388624 | tf_op jit(solution)/shard_map/all_gather | solution.py:191
  1056.2 209.3 %while.29 = (s32[]{:T(128)}, f32[2048,4,128]{0,2,1:T(8,128)}, f32[2048,4,128]{0,2,1:T(8,128)}, bf16[4,512,4,128]{3,1,2,0:T(8,128)(2,1)}, bf16[4,512,4,128]{3,1,2...) while((s32[]{:T(128)}, f32[2048,4,128]{0,2,1:T(8,128)}, ...), condition=%wide.region_17.18_spmd.clone, body=%wide.region_15.17_spmd.clone.sunk | while | flops 5437390848 | bytes 253296880 | solution.py:225
  1073.9 12.4 multiply_reduce_fusion.9
  1086.3 12.4 multiply_convert_fusion.6
  1138.8 12.9 multiply_convert_fusion.6
  1179.6 12.4 multiply_reduce_fusion.9
  1317.2 12.7 fusion.68
  1338.3 17.1 %add_convert_fusion = bf16[2048,2048]{1,0:T(8,128)(2,1)} fusion(f32[2048,2048]{1,0:T(8,128)} %fusion.50, f32[2048,2048]{1,0:T(8,128)} %fusion.68, bf16[2048,512]{0,1:T(8,128)(2,1)S(1)} %bitcast.145, bf16[2048,512]{1,0:T(8,128)(2,1)} %all-gather.16.cloned.1.call-done), kind=kOutput, calls=%fused_computation.58 | convolution fusion | flops 4307550208 | bytes 46137344 | tf_op jit(solution)/shard_map/dot_general | solution.py:26
  1361.0 37.2 %all-reduce.12.cloned.1.call-done = (f32[2048]{0:T(1024)}, f32[2048]{0:T(1024)}, f32[2048]{0:T(1024)}, f32[2048]{0:T(1024)}, f32[2048]{0:T(1024)}, /*index=5*/f3...) async-done(((f32[2048]{0:T(1024)}, f32[2048]{0:T(1024)}, f32[2048]{0:T(1024)}, f32[2048]{0:T(1024)}, f32[2048]{0:T(1024)}, /*index=5*/f32[8192]{0:T(1024)}, ...) | async-done | bytes 98320
  1409.6 28.0 %reduce-scatter.25.cloned.1.call-done = bf16[256,512]{1,0:T(8,128)(2,1)} async-done(((bf16[2048,512]{1,0:T(8,128)(2,1)}), bf16[256,512]{1,0:T(8,128)(2,1)}) %reduce-scatter.25.cloned.1.call-update) | async-done | bytes 262160 | tf_op jit(solution)/shard_map/reduce_scatter | solution.py:257
  1439.3 35.6 %reduce-scatter.19.cloned.1.call-done = bf16[256,512]{0,1:T(8,128)(2,1)} async-done(((bf16[2048,512]{0,1:T(8,128)(2,1)}), bf16[256,512]{0,1:T(8,128)(2,1)}) %reduce-scatter.19.cloned.1.call-update) | async-done | bytes 262160 | tf_op jit(solution)/shard_map/reduce_scatter | solution.py:248
  1476.8 34.9 %reduce-scatter.21.cloned.1.call-done = bf16[256,512]{0,1:T(8,128)(2,1)} async-done(((bf16[2048,512]{0,1:T(8,128)(2,1)}), bf16[256,512]{0,1:T(8,128)(2,1)}) %reduce-scatter.21.cloned.1.call-update) | async-done | bytes 262160 | tf_op jit(solution)/shard_map/reduce_scatter | solution.py:251
  1513.6 35.0 %reduce-scatter.23.cloned.1.call-done = bf16[256,512]{0,1:T(8,128)(2,1)} async-done(((bf16[2048,512]{0,1:T(8,128)(2,1)}), bf16[256,512]{0,1:T(8,128)(2,1)}) %reduce-scatter.23.cloned.1.call-update) | async-done | bytes 262160 | tf_op jit(solution)/shard_map/reduce_scatter | solution.py:254
  1550.6 85.9 %reduce-scatter.17.cloned.1.call-done = bf16[512,2048]{1,0:T(8,128)(2,1)} async-done(((bf16[2048,2048]{1,0:T(8,128)(2,1)}), bf16[512,2048]{1,0:T(8,128)(2,1)}) %reduce-scatter.17.cloned.1.call-update) | async-done | bytes 2097168 | tf_op jit(solution)/shard_map/reduce_scatter | solution.py:240
  (264 shorter events, 472.8 us)
Async XLA Ops:
  7.2 34.3 %all-gather.16.cloned.1.call-start = ((), (), s32[]{:S(2)}) async-start(), calls=%async_computation.13 | async-start | bytes 2359296 | tf_op jit(solution)/shard_map/all_gather | solution.py:95
  7.9 122.3 %all-gather.10.cloned.1.call-start = ((), (), s32[]{:S(2)}) async-start(), calls=%async_computation.10 | async-start | bytes 10485760 | tf_op jit(solution)/shard_map/all_gather | solution.py:98
  8.7 152.4 %all-gather.12.cloned.1.call-start = ((), (), s32[]{:S(2)}) async-start(), calls=%async_computation.11 | async-start | bytes 2359296 | tf_op jit(solution)/shard_map/all_gather | solution.py:93
  9.4 181.7 %all-gather.14.cloned.1.call-start = ((), (), s32[]{:S(2)}) async-start(), calls=%async_computation.12 | async-start | bytes 2359296 | tf_op jit(solution)/shard_map/all_gather | solution.py:94
  10.0 281.0 %all-gather.18.cloned.1.call-start = ((), (), s32[]{:S(2)}) async-start(), calls=%async_computation.14 | async-start | bytes 2359296 | tf_op jit(solution)/shard_map/all_gather | solution.py:96
  10.6 377.2 %reduce-scatter.11.cloned.1.call-start = ((), (), s32[]{:S(2)}) async-start(), calls=%async_computation.15 | async-start | bytes 10485760 | tf_op jit(solution)/shard_map/reduce_scatter | solution.py:130
  291.0 10.8 copy-start.2
  301.8 85.9 %copy-start.7 = (bf16[512,2048]{1,0:T(8,128)(2,1)S(1)}, bf16[512,2048]{1,0:T(8,128)(2,1)}, u32[]{:S(2)}) copy-start(bf16[512,2048]{1,0:T(8,128)(2,1)} %param.22) | copy-start | bytes 6291460
  301.8 85.9 %copy-start.17 = (f32[2048]{0:T(1024)S(1)}, f32[2048]{0:T(1024)}, u32[]{:S(2)}) copy-start(f32[2048]{0:T(1024)} %param.33) | copy-start | bytes 24580
  301.9 256.5 %all-gather.20.cloned.1.call-start = ((), (), s32[]{:S(2)}) async-start(), calls=%async_computation.16 | async-start | bytes 9437184 | tf_op jit(solution)/shard_map/all_gather | solution.py:141
  302.6 280.0 %all-gather.22.cloned.1.call-start = ((), (), s32[]{:S(2)}) async-start(), calls=%async_computation.17 | async-start | bytes 9437184 | tf_op jit(solution)/shard_map/all_gather | solution.py:142
  303.4 88.0 %copy-start.18 = (f32[2048]{0:T(1024)S(1)}, f32[2048]{0:T(1024)}, u32[]{:S(2)}) copy-start(f32[2048]{0:T(1024)} %param.34) | copy-start | bytes 24580
  303.4 88.0 %copy-start.22 = (f32[2048]{0:T(1024)S(1)}, f32[2048]{0:T(1024)}, u32[]{:S(2)}) copy-start(f32[2048]{0:T(1024)} %param.35) | copy-start | bytes 24580
  303.4 392.3 %reduce-scatter.13.cloned.1.call-start = ((), (), s32[]{:S(2)}) async-start(), calls=%async_computation.18 | async-start | bytes 10485760 | tf_op jit(solution)/shard_map/reduce_scatter | solution.py:160
  393.9 49.7 %collective-permute-start = (bf16[512,2048]{1,0:T(8,128)(2,1)}, bf16[512,2048]{1,0:T(8,128)(2,1)}, u32[]{:S(2)}, u32[]{:S(2)}) collective-permute-start(bf16[512,2048]{1,0:T(8,128)(2,1)} %fusion.44), channel_id=1, source_target_pairs={{0,1},{1,2},{2,3},{3,0},{4,5},{5,6},{6,7},{7,4},{8,9},{9,10},{10,1... | collective-permute-start | bytes 6291464 | tf_op jit(solution)/shard_map/ppermute | solution.py:150
  395.4 93.2 %collective-permute-start.2 = (bf16[512,2048]{1,0:T(8,128)(2,1)}, bf16[512,2048]{1,0:T(8,128)(2,1)}, u32[]{:S(2)}, u32[]{:S(2)}) collective-permute-start(bf16[512,2048]{1,0:T(8,128)(2,1)} %fusion.44), channel_id=1, source_target_pairs={{1,0},{2,1},{3,2},{0,3},{5,4},{6,5},{7,6},{4,7},{9,8},{10,9},{11,1... | collective-permute-start | bytes 6291464 | tf_op jit(solution)/shard_map/ppermute | solution.py:152
  443.6 88.6 %collective-permute-start.1 = (bf16[512,2048]{1,0:T(8,128)(2,1)}, bf16[512,2048]{1,0:T(8,128)(2,1)}, u32[]{:S(2)}, u32[]{:S(2)}) collective-permute-start(bf16[512,2048]{1,0:T(8,128)(2,1)} %collective-permute-done), channel_id=1, source_target_pairs={{0,1},{1,2},{2,3},{3,0},{4,5},{5,6},{6,7},{7,4},{8,9},{9,10},{10,1... | collective-permute-start | bytes 6291464 | tf_op jit(solution)/shard_map/ppermute | solution.py:150
  609.2 86.6 %copy-start.24 = (f32[2048]{0:T(1024)S(1)}, f32[2048]{0:T(1024)}, u32[]{:S(2)}) copy-start(f32[2048]{0:T(1024)} %param.37) | copy-start | bytes 24580
  609.2 186.8 %all-gather.24.cloned.1.call-start = ((), (), s32[]{:S(2)}) async-start(), calls=%async_computation.19 | async-start | bytes 10485760 | tf_op jit(solution)/shard_map/all_gather | solution.py:173
  708.4 233.2 %reduce-scatter.15.cloned.1.call-start = ((), (), s32[]{:S(2)}) async-start(), calls=%async_computation.20 | async-start | bytes 10485760 | tf_op jit(solution)/shard_map/reduce_scatter | solution.py:181
  855.2 187.8 %all-gather.26.cloned.1.call-start = ((), (), s32[]{:S(2)}) async-start(), calls=%async_computation.21 | async-start | bytes 10485760 | tf_op jit(solution)/shard_map/all_gather | solution.py:191
  955.3 400.1 %reduce-scatter.29.cloned.1.call-start = ((), (), s32[]{:S(2)}) async-start(), calls=%async_computation.28 | async-start | bytes 9437184 | tf_op jit(solution)/shard_map/reduce_scatter | solution.py:263
  980.5 377.7 %reduce-scatter.27.cloned.1.call-start = ((), (), s32[]{:S(2)}) async-start(), calls=%async_computation.27 | async-start | bytes 9437184 | tf_op jit(solution)/shard_map/reduce_scatter | solution.py:260
  1006.4 36.5 %copy-start.26 = (bf16[2048,512]{1,0:T(8,128)(2,1)S(1)}, bf16[2048,512]{1,0:T(8,128)(2,1)}, u32[]{:S(2)}) copy-start(bf16[2048,512]{1,0:T(8,128)(2,1)} %all-gather.18.cloned.1.call-done) | copy-start | bytes 6291460
  1006.5 391.7 %all-reduce.12.cloned.1.call-start = ((), (), s32[]{:S(2)}) async-start(), calls=%async_computation.29 | async-start | bytes 196608
  1270.8 166.8 %reduce-scatter.25.cloned.1.call-start = ((), (), s32[]{:S(2)}) async-start(), calls=%async_computation.26 | async-start | bytes 2359296 | tf_op jit(solution)/shard_map/reduce_scatter | solution.py:257
  1280.7 194.3 %reduce-scatter.19.cloned.1.call-start = ((), (), s32[]{:S(2)}) async-start(), calls=%async_computation.23 | async-start | bytes 2359296 | tf_op jit(solution)/shard_map/reduce_scatter | solution.py:248
  1294.5 217.2 %reduce-scatter.21.cloned.1.call-start = ((), (), s32[]{:S(2)}) async-start(), calls=%async_computation.24 | async-start | bytes 2359296 | tf_op jit(solution)/shard_map/reduce_scatter | solution.py:251
  1307.6 241.1 %reduce-scatter.23.cloned.1.call-start = ((), (), s32[]{:S(2)}) async-start(), calls=%async_computation.25 | async-start | bytes 2359296 | tf_op jit(solution)/shard_map/reduce_scatter | solution.py:254
  1317.2 319.3 %reduce-scatter.17.cloned.1.call-start = ((), (), s32[]{:S(2)}) async-start(), calls=%async_computation.22 | async-start | bytes 10485760 | tf_op jit(solution)/shard_map/reduce_scatter | solution.py:240
  1317.2 12.7 copy-start.16
  1317.2 12.7 copy-start.25
  (34 other events, 143.0 us)
Sparse Core Ops, SparseCore 0:
  9.6 31.8 all-gather.15
  43.3 86.8 all-gather.9
  131.9 29.1 all-gather.11
  162.5 28.5 all-gather.13
  192.5 28.5 all-gather.17
  302.0 85.7 reduce-scatter.10
  389.3 82.0 all-gather.19
  473.0 80.5 all-gather.21
  609.3 86.3 reduce-scatter.12
  708.5 87.4 all-gather.23
  855.3 86.2 reduce-scatter.14
  955.4 87.4 all-gather.25
  1045.2 89.5 reduce-scatter.28
  1137.0 87.9 reduce-scatter.26
  1270.9 127.2 all-reduce.11
  1400.3 37.1 reduce-scatter.24
  1440.2 34.6 reduce-scatter.18
  1477.1 34.5 reduce-scatter.20
  1514.0 34.5 reduce-scatter.22
  1551.6 84.8 reduce-scatter.16
